TPU v7x, 32 devices: a whole 2x2x4 slice. The times are simulated.
32 devices in a mesh: tile: 8 (over y, x, core), frame: 4 (over z).
Axes of the slice: x: 2, y: 2, z: 4, core: 2. Of those that a mesh axis runs over, the one named last changes fastest.
Arguments:
- video: float32 [16, 16, 160, 128], P('frame', 'tile'), may hold values from -6 to 6
- norm_gain: float32 [2, 2, 128], replicated, may hold values from 0.1 to 1.9
- space_weight: float32 [2, 3, 3, 128, 128], replicated, may hold values from -0.1875 to 0.1875
- time_weight: float32 [2, 3, 128, 128], replicated, may hold values from -0.3125 to 0.3125
- down_weight: float32 [3, 3, 128, 256], replicated, may hold values from -0.1875 to 0.1875
- attn_gain: float32 [256], replicated, may hold values from 0.1 to 1.9
- w_query: float32 [256, 256], replicated, may hold values from -4 to 4
- w_key: float32 [256, 256], replicated, may hold values from -4 to 4
- w_value: float32 [256, 256], replicated, may hold values from -0.375 to 0.375
- w_out: float32 [256, 256], replicated, may hold values from -0.375 to 0.375
Outputs:
- encoded: float32 [32, 320, 256], P(('frame', 'tile'))
All inputs are finite; a program needn't handle non-finite values.
Results may differ from a plain program's by a relative error of at most 0.0003.
Values sent between devices are 32-bit elements; how exact they have to be, the bound alone decides.
No kernel may reach another device: no remote copies, remote signals or barrier semaphores. Data moves between devices by JAX's collectives and lax.ppermute only.
A program may use at most 64 MiB of HBM per device.

v0:
```python
import jax
import jax.numpy as jnp
from jax import lax
from jax.sharding import PartitionSpec as P

highest = lax.Precision.HIGHEST


def passed_along(shard, axis, by):
    size = lax.axis_size(axis)
    pairs = [(i, i + by) for i in range(size) if 0 <= i + by < size]
    return lax.ppermute(shard, axis, pairs)


def extended(cells, sides, width):
    for axis, dim in sides:
        count = lax.axis_size(axis)
        ends = count - 1
        head = lax.slice_in_dim(cells, 0, width, axis=dim)
        tail = lax.slice_in_dim(cells, cells.shape[dim] - width, cells.shape[dim], axis=dim)
        cells = jnp.concatenate(
            [
                lax.ppermute(tail, axis, [(i, (i + 1) % count) for i in range(ends)]),
                cells,
                lax.ppermute(head, axis, [((i + 1) % count, i) for i in range(ends)]),
            ],
            axis=dim,
        )
    return cells


def from_partner(shard, axis, apart):
    return lax.ppermute(shard, axis, [(i, i ^ 1 << apart) for i in range(lax.axis_size(axis))])


def norm(values, gain):
    return values * lax.rsqrt(jnp.mean(values * values, -1, keepdims=True) + 1e-06) * gain


def act(values, gain):
    return jax.nn.silu(norm(values, gain))


def conv_rows(inputs, kernel):
    return lax.conv_general_dilated(
        inputs,
        kernel,
        (1, 1),
        ((0, 0), (1, 1)),
        dimension_numbers=("NHWC", "HWIO", "NHWC"),
        precision=highest,
    )


def time_mix(inputs, kernel):
    earlier = passed_along(inputs[-2:], "frame", 1)
    opening = lax.axis_index("frame") == 0
    start = jnp.where(opening, jnp.concatenate([inputs[:1], inputs[:1]], 0), earlier)
    padded = jnp.concatenate([start, inputs], 0)
    count = inputs.shape[0]
    total = jnp.einsum("fhwc,cd->fhwd", padded[0:count], kernel[0], precision=highest)
    total = total + jnp.einsum("fhwc,cd->fhwd", padded[1 : count + 1], kernel[1], precision=highest)
    total = total + jnp.einsum("fhwc,cd->fhwd", padded[2 : count + 2], kernel[2], precision=highest)
    return total


def fold(carry, query, keys, values):
    best, total, accum = carry
    scores = jnp.dot(query, keys.T, precision=highest)
    new_best = jnp.maximum(best, jnp.max(scores, axis=1))
    factor = jnp.exp(best - new_best)
    weights = jnp.exp(scores - new_best[:, None])
    total = total * factor + jnp.sum(weights, axis=1)
    accum = accum * factor[:, None] + jnp.dot(weights, values, precision=highest)
    return (new_best, total, accum)


def local(
    video,
    norm_gain,
    space_weight,
    time_weight,
    down_weight,
    attn_gain,
    w_query,
    w_key,
    w_value,
    w_out,
):
    frames_dev, rows, width, chans = video.shape
    tiles = lax.axis_size("tile")
    state = video
    for block in range(2):
        wide = extended(act(state, norm_gain[block, 0]), (("tile", 1),), 1)
        mixed = conv_rows(wide, space_weight[block])
        state = state + time_mix(act(mixed, norm_gain[block, 1]), time_weight[block])
    upper = passed_along(state[:, -1:], "tile", 1)
    stacked = jnp.concatenate([upper, state], 1)
    lowered = lax.conv_general_dilated(
        stacked,
        down_weight,
        (2, 2),
        ((0, 0), (1, 0)),
        dimension_numbers=("NHWC", "HWIO", "NHWC"),
        precision=highest,
    )
    outer = lowered.shape[-1]
    group = tiles // frames_dev
    pieces = lowered.reshape(frames_dev * group, -1, outer)
    mine = lax.all_to_all(pieces, "tile", split_axis=0, concat_axis=0, tiled=True).reshape(
        -1, outer
    )
    normed = norm(mine, attn_gain)
    query = jnp.dot(normed, w_query, precision=highest) * float(outer) ** (-0.5)
    count = mine.shape[0]
    carry = (
        jnp.full((count,), -jnp.inf, jnp.float32),
        jnp.zeros((count,), jnp.float32),
        jnp.zeros((count, outer), jnp.float32),
    )
    levels = group.bit_length() - 1
    keys = jnp.dot(normed, w_key, precision=highest)
    values = jnp.dot(normed, w_value, precision=highest)
    carry = fold(carry, query, keys, values)
    for level in range(levels):
        got_keys, got_values = from_partner((keys, values), "tile", level)
        carry = fold(carry, query, got_keys, got_values)
        keys = jnp.concatenate([keys, got_keys], 0)
        values = jnp.concatenate([values, got_values], 0)
    best, total, accum = carry
    attended = accum / total[:, None]
    result = mine + jnp.dot(attended, w_out, precision=highest)
    return result[None]


def solution(mesh):
    in_specs = (P("frame", "tile", None, None), P(), P(), P(), P(), P(), P(), P(), P(), P())
    out_specs = P(("frame", "tile"), None, None)
    return jax.shard_map(local, mesh=mesh, in_specs=in_specs, out_specs=out_specs, check_vma=False)
```

profile of v0, /device:TPU:0, one launch (start us, length us, event | category | flops | bytes accessed | tf_op | source)
XLA Modules:
  0.0 101.9 jit_solution(15611979728672710645)
XLA Ops:
  0.0 0.8 slice_bitcast_fusion.2
  0.8 1.4 %multiply_reduce_fusion.3 = f32[4,2,160]{2,1,0:T(2,128)S(1)} fusion(f32[4,2,160,128]{3,2,1,0:T(8,128)} %param.10), kind=kLoop, calls=%fused_computation.49 | loop fusion | flops 326400 | bytes 660480 | tf_op jit(solution)/shard_map/reduce_sum | solution.py:37
  2.3 1.3 %divide_multiply_fusion.3 = f32[4,2,160,128]{3,2,1,0:T(8,128)S(1)} fusion(f32[4,2,160,128]{3,2,1,0:T(8,128)} %param.10, f32[128]{0:T(128)S(1)} %get-tuple-element.14, f32[4,2,160]{2,1,0:T(2,128)S(1)} %add_rsqrt_fusion.3), kind=kLoop, calls=%fused_computation.48 | loop fusion | flops 983040 | bytes 1316352 | tf_op jit(solution)/shard_map/jit(silu)/mul | solution.py:41
  3.7 2.4 %collective-permute-start = (f32[4,1,160,128]{3,2,1,0:T(8,128)S(1)}, f32[4,1,160,128]{3,2,1,0:T(8,128)S(1)}, u32[]{:S(2)}, u32[]{:S(2)}) collective-permute-start(f32[4,1,160,128]{3,2,1,0:T(8,128)S(1)} %get-tuple-element.9), channel_id=1, source_target_pairs={{0,4},{4,8},{8,12},{12,16},{16,20},{20,24},{24,28},{1,5},{5,9},{9,... | collective-permute-start | bytes 983048 | tf_op jit(solution)/shard_map/ppermute | solution.py:23
  6.1 1.3 %collective-permute-start.1 = (f32[4,1,160,128]{3,2,1,0:T(8,128)S(1)}, f32[4,1,160,128]{3,2,1,0:T(8,128)S(1)}, u32[]{:S(2)}, u32[]{:S(2)}) collective-permute-start(f32[4,1,160,128]{3,2,1,0:T(8,128)S(1)} %get-tuple-element.10), channel_id=1, source_target_pairs={{4,0},{8,4},{12,8},{16,12},{20,16},{24,20},{28,24},{5,1},{9,5},{13... | collective-permute-start | bytes 983048 | tf_op jit(solution)/shard_map/ppermute | solution.py:25
  7.4 4.3 %collective-permute-done.1 = f32[4,1,160,128]{3,2,1,0:T(8,128)S(1)} collective-permute-done((f32[4,1,160,128]{3,2,1,0:T(8,128)S(1)}, f32[4,1,160,128]{3,2,1,0:T(8,128)S(1)}, u32[]{:S(2)}, u32[]{:S(2)}) %collective-permute-start.1) | collective-permute-done | bytes 327712 | tf_op jit(solution)/shard_map/ppermute | solution.py:25
  11.8 0.8 copy.52
  13.0 0.3 select_maximum_fusion.1
  13.3 0.9 copy-done.2
  14.2 5.3 %multiply_reduce_fusion.1 = (f32[2,32,21]{1,2,0:T(8,128)S(1)}, f32[2,32,21,128]{3,1,2,0:T(8,128)S(1)}) fusion(f32[2,3,3,128,128]{4,3,2,1,0:T(8,128)S(1)} %copy-done.2, f32[4,4,8,23,128]{4,1,3,2,0:T(4,128)S(1)} %select_maximum_fusion.1, pred[32,21]{0,1:T(8,128)(4,1)S(1)} %copy-done.10), kind=kOutput, calls=%fused_computation.37 | convolution fusion | flops 2378685184 | bytes 2793728 | tf_op jit(solution)/shard_map/conv_general_dilated | solution.py:45
  19.7 0.5 copy.30
  20.6 3.5 %collective-permute-start.2 = (f32[2,2,160,128]{3,2,1,0:T(8,128)S(1)}, f32[2,2,160,128]{3,2,1,0:T(8,128)S(1)}, u32[]{:S(2)}, u32[]{:S(2)}) collective-permute-start(f32[2,2,160,128]{3,2,1,0:T(8,128)S(1)} %slice.130), channel_id=1, source_target_pairs={{0,1},{1,2},{2,3},{4,5},{5,6},{6,7},{8,9},{9,10},{10,11},{12,13},{... | collective-permute-start | bytes 983048 | tf_op jit(solution)/shard_map/ppermute | solution.py:12
  24.2 0.7 fusion.40
  24.9 3.8 %collective-permute-done.2 = f32[2,2,160,128]{3,2,1,0:T(8,128)S(1)} collective-permute-done((f32[2,2,160,128]{3,2,1,0:T(8,128)S(1)}, f32[2,2,160,128]{3,2,1,0:T(8,128)S(1)}, u32[]{:S(2)}, u32[]{:S(2)}) %collective-permute-start.2) | collective-permute-done | bytes 327712 | tf_op jit(solution)/shard_map/ppermute | solution.py:12
  28.7 0.7 fusion.22
  29.4 0.9 multiply_reduce_fusion.2
  30.3 0.3 divide_multiply_fusion.1
  30.6 7.2 %collective-permute-start.3 = (f32[4,1,160,128]{3,2,1,0:T(8,128)S(1)}, f32[4,1,160,128]{3,2,1,0:T(8,128)S(1)}, u32[]{:S(2)}, u32[]{:S(2)}) collective-permute-start(f32[4,1,160,128]{3,2,1,0:T(8,128)S(1)} %get-tuple-element.7), channel_id=1, source_target_pairs={{0,4},{4,8},{8,12},{12,16},{16,20},{20,24},{24,28},{1,5},{5,9},{9,... | collective-permute-start | bytes 983048 | tf_op jit(solution)/shard_map/ppermute | solution.py:23
  37.8 1.5 %collective-permute-start.4 = (f32[4,1,160,128]{3,2,1,0:T(8,128)S(1)}, f32[4,1,160,128]{3,2,1,0:T(8,128)S(1)}, u32[]{:S(2)}, u32[]{:S(2)}) collective-permute-start(f32[4,1,160,128]{3,2,1,0:T(8,128)S(1)} %get-tuple-element.8), channel_id=1, source_target_pairs={{4,0},{8,4},{12,8},{16,12},{20,16},{24,20},{28,24},{5,1},{9,5},{13... | collective-permute-start | bytes 983048 | tf_op jit(solution)/shard_map/ppermute | solution.py:25
  39.3 4.8 %collective-permute-done.4 = f32[4,1,160,128]{3,2,1,0:T(8,128)S(1)} collective-permute-done((f32[4,1,160,128]{3,2,1,0:T(8,128)S(1)}, f32[4,1,160,128]{3,2,1,0:T(8,128)S(1)}, u32[]{:S(2)}, u32[]{:S(2)}) %collective-permute-start.4) | collective-permute-done | bytes 327712 | tf_op jit(solution)/shard_map/ppermute | solution.py:25
  44.2 0.8 copy.53
  45.3 0.3 select_maximum_fusion
  45.7 0.9 copy-done.3
  46.6 5.3 %multiply_reduce_fusion = (f32[2,32,21]{1,2,0:T(8,128)S(1)}, f32[2,32,21,128]{3,1,2,0:T(8,128)S(1)}) fusion(f32[2,3,3,128,128]{4,3,2,1,0:T(8,128)S(1)} %copy-done.3, f32[4,4,8,23,128]{4,1,3,2,0:T(4,128)S(1)} %select_maximum_fusion, pred[32,21]{0,1:T(8,128)(4,1)S(1)} %copy-done.10), kind=kOutput, calls=%fused_computation.36 | convolution fusion | flops 2378685184 | bytes 2793728 | tf_op jit(solution)/shard_map/conv_general_dilated | solution.py:45
  52.1 0.5 copy.36
  52.7 0.3 divide_multiply_fusion
  53.0 4.4 %collective-permute-start.5 = (f32[2,2,160,128]{3,2,1,0:T(8,128)S(1)}, f32[2,2,160,128]{3,2,1,0:T(8,128)S(1)}, u32[]{:S(2)}, u32[]{:S(2)}) collective-permute-start(f32[2,2,160,128]{3,2,1,0:T(8,128)S(1)} %slice.137), channel_id=1, source_target_pairs={{0,1},{1,2},{2,3},{4,5},{5,6},{6,7},{8,9},{9,10},{10,11},{12,13},{... | collective-permute-start | bytes 983048 | tf_op jit(solution)/shard_map/ppermute | solution.py:12
  57.5 0.7 fusion.36
  58.1 3.9 %collective-permute-done.5 = f32[2,2,160,128]{3,2,1,0:T(8,128)S(1)} collective-permute-done((f32[2,2,160,128]{3,2,1,0:T(8,128)S(1)}, f32[2,2,160,128]{3,2,1,0:T(8,128)S(1)}, u32[]{:S(2)}, u32[]{:S(2)}) %collective-permute-start.5) | collective-permute-done | bytes 327712 | tf_op jit(solution)/shard_map/ppermute | solution.py:12
  62.0 0.7 fusion.21
  62.7 0.7 fusion.15
  63.4 8.4 %collective-permute-start.6 = (f32[4,1,160,128]{3,2,1,0:T(8,128)S(1)}, f32[4,1,160,128]{3,2,1,0:T(8,128)S(1)}, u32[]{:S(2)}, u32[]{:S(2)}) collective-permute-start(f32[4,1,160,128]{3,2,1,0:T(8,128)S(1)} %slice.138), channel_id=1, source_target_pairs={{0,4},{4,8},{8,12},{12,16},{16,20},{20,24},{24,28},{1,5},{5,9},{9,... | collective-permute-start | bytes 983048 | tf_op jit(solution)/shard_map/ppermute | solution.py:12
  71.8 1.0 collective-permute-done.6
  72.9 0.6 copy.54
  73.7 0.3 select_maximum_fusion.2
  74.0 0.3 copy-done.11
  74.4 1.7 %convolution_select_fusion = f32[1,32,11,256]{3,1,2,0:T(8,128)S(1)} fusion(f32[3,3,128,256]{3,2,1,0:T(8,128)S(1)} %copy-done, f32[3,4,8,24,128]{4,1,3,2,0:T(4,128)S(1)} %select_maximum_fusion.2, pred[32,11]{0,1:T(8,128)(4,1)S(1)} %copy-done.11), kind=kOutput, calls=%fused_computation.19 | convolution fusion | flops 1245798400 | bytes 2720096 | tf_op jit(solution)/shard_map/conv_general_dilated | solution.py:99
  76.1 0.4 copy.42
  76.8 17.8 %all_to_all.5 = f32[8,40,256]{2,1,0:T(8,128)S(1)} all-to-all(f32[8,40,256]{2,1,0:T(8,128)S(1)} %bitcast.145), channel_id=1, replica_groups=mesh['tile'=8,'frame'=4] {'tile'}, dimensions={0} | all-to-all | bytes 655360 | tf_op jit(solution)/shard_map/all_to_all | solution.py:110
  95.0 0.4 fusion.59
  95.4 0.4 fusion.58
  95.9 0.4 convolution_multiply_fusion
  96.4 0.6 collective-permute-start.8
  96.9 0.7 fusion.56
  97.6 0.7 fusion.57
  98.6 1.1 %fusion.17 = f32[320,256]{1,0:T(8,128)S(1)} fusion(f32[320,256]{1,0:T(8,128)S(1)} %fusion.59, f32[320,320]{0,1:T(8,128)S(1)} %get-tuple-element.23, f32[320]{0:T(512)S(1)} %get-tuple-element.22, f32[320]{0:T(512)S(1)} %get-tuple-element.6, f32[320]{0:T(512)S(1)} %get-tuple-element.11), kind=kOutput, calls=%fused_computation.25 | convolution fusion | flops 314839040 | bytes 1068800 | tf_op jit(solution)/shard_map/dot_general | solution.py:74
  99.7 1.1 %fusion.18 = f32[320,256]{1,0:T(8,128)S(1)} fusion(f32[320,256]{1,0:T(8,128)S(1)} %fusion.17, f32[320,256]{1,0:T(8,128)S(1)} %collective-permute-done.8, f32[320,320]{0,1:T(8,128)S(1)} %get-tuple-element.25, f32[320]{0:T(512)S(1)} %max.13, f32[320]{0:T(512)S(1)} %get-tuple-element.5), kind=kOutput, calls=%fused_computation.26 | convolution fusion | flops 314839040 | bytes 1395200 | tf_op jit(solution)/shard_map/dot_general | solution.py:74
  100.8 1.2 %fusion.16 = f32[1,320,256]{2,1,0:T(8,128)} fusion(f32[320,256]{1,0:T(8,128)S(1)} %bitcast.139, f32[320,256]{1,0:T(8,128)S(1)} %fusion.18, f32[256,256]{1,0:T(8,128)S(1)} %copy-done.9), kind=kOutput, calls=%fused_computation.21 | convolution fusion | flops 251740160 | bytes 1245184 | tf_op jit(solution)/shard_map/dot_general | solution.py:132
  (70 shorter events, 2.8 us)
Async XLA Ops:
  0.0 74.0 %copy-start = (f32[3,3,128,256]{3,2,1,0:T(8,128)S(1)}, f32[3,3,128,256]{3,2,1,0:T(8,128)}, u32[]{:S(2)}) copy-start(f32[3,3,128,256]{3,2,1,0:T(8,128)} %param.14) | copy-start | bytes 3538948
  3.7 3.7 %collective-permute-start = (f32[4,1,160,128]{3,2,1,0:T(8,128)S(1)}, f32[4,1,160,128]{3,2,1,0:T(8,128)S(1)}, u32[]{:S(2)}, u32[]{:S(2)}) collective-permute-start(f32[4,1,160,128]{3,2,1,0:T(8,128)S(1)} %get-tuple-element.9), channel_id=1, source_target_pairs={{0,4},{4,8},{8,12},{12,16},{16,20},{20,24},{24,28},{1,5},{5,9},{9,... | collective-permute-start | bytes 983048 | tf_op jit(solution)/shard_map/ppermute | solution.py:23
  6.1 5.6 %collective-permute-start.1 = (f32[4,1,160,128]{3,2,1,0:T(8,128)S(1)}, f32[4,1,160,128]{3,2,1,0:T(8,128)S(1)}, u32[]{:S(2)}, u32[]{:S(2)}) collective-permute-start(f32[4,1,160,128]{3,2,1,0:T(8,128)S(1)} %get-tuple-element.10), channel_id=1, source_target_pairs={{4,0},{8,4},{12,8},{16,12},{20,16},{24,20},{28,24},{5,1},{9,5},{13... | collective-permute-start | bytes 983048 | tf_op jit(solution)/shard_map/ppermute | solution.py:25
  12.9 1.3 %copy-start.2 = (f32[2,3,3,128,128]{4,3,2,1,0:T(8,128)S(1)}, f32[2,3,3,128,128]{4,3,2,1,0:T(8,128)}, u32[]{:S(2)}) copy-start(f32[2,3,3,128,128]{4,3,2,1,0:T(8,128)} %param.12) | copy-start | bytes 3538948
  12.9 1.3 %copy-start.10 = (pred[32,21]{0,1:T(8,128)(4,1)S(1)}, pred[32,21]{0,1:T(8,128)(4,1)}, u32[]{:S(2)}) copy-start(pred[32,21]{0,1:T(8,128)(4,1)} %constant.47) | copy-start | bytes 2020
  20.3 3.8 %copy-start.4 = (f32[2,3,128,128]{3,2,1,0:T(8,128)S(1)}, f32[2,3,128,128]{3,2,1,0:T(8,128)}, u32[]{:S(2)}) copy-start(f32[2,3,128,128]{3,2,1,0:T(8,128)} %param.13) | copy-start | bytes 1179652
  20.6 8.1 %collective-permute-start.2 = (f32[2,2,160,128]{3,2,1,0:T(8,128)S(1)}, f32[2,2,160,128]{3,2,1,0:T(8,128)S(1)}, u32[]{:S(2)}, u32[]{:S(2)}) collective-permute-start(f32[2,2,160,128]{3,2,1,0:T(8,128)S(1)} %slice.130), channel_id=1, source_target_pairs={{0,1},{1,2},{2,3},{4,5},{5,6},{6,7},{8,9},{9,10},{10,11},{12,13},{... | collective-permute-start | bytes 983048 | tf_op jit(solution)/shard_map/ppermute | solution.py:12
  24.8 4.6 %copy-start.1 = (f32[4,2,160,128]{3,2,1,0:T(8,128)S(1)}, f32[4,2,160,128]{3,2,1,0:T(8,128)}, u32[]{:S(2)}) copy-start(f32[4,2,160,128]{3,2,1,0:T(8,128)} %param.10) | copy-start | bytes 1966084
  30.6 8.7 %collective-permute-start.3 = (f32[4,1,160,128]{3,2,1,0:T(8,128)S(1)}, f32[4,1,160,128]{3,2,1,0:T(8,128)S(1)}, u32[]{:S(2)}, u32[]{:S(2)}) collective-permute-start(f32[4,1,160,128]{3,2,1,0:T(8,128)S(1)} %get-tuple-element.7), channel_id=1, source_target_pairs={{0,4},{4,8},{8,12},{12,16},{16,20},{20,24},{24,28},{1,5},{5,9},{9,... | collective-permute-start | bytes 983048 | tf_op jit(solution)/shard_map/ppermute | solution.py:23
  37.8 6.3 %collective-permute-start.4 = (f32[4,1,160,128]{3,2,1,0:T(8,128)S(1)}, f32[4,1,160,128]{3,2,1,0:T(8,128)S(1)}, u32[]{:S(2)}, u32[]{:S(2)}) collective-permute-start(f32[4,1,160,128]{3,2,1,0:T(8,128)S(1)} %get-tuple-element.8), channel_id=1, source_target_pairs={{4,0},{8,4},{12,8},{16,12},{20,16},{24,20},{28,24},{5,1},{9,5},{13... | collective-permute-start | bytes 983048 | tf_op jit(solution)/shard_map/ppermute | solution.py:25
  45.3 1.3 %copy-start.3 = (f32[2,3,3,128,128]{4,3,2,1,0:T(8,128)S(1)}, f32[2,3,3,128,128]{4,3,2,1,0:T(8,128)}, u32[]{:S(2)}) copy-start(f32[2,3,3,128,128]{4,3,2,1,0:T(8,128)} %param.12) | copy-start | bytes 3538948
  52.7 4.7 %copy-start.5 = (f32[2,3,128,128]{3,2,1,0:T(8,128)S(1)}, f32[2,3,128,128]{3,2,1,0:T(8,128)}, u32[]{:S(2)}) copy-start(f32[2,3,128,128]{3,2,1,0:T(8,128)} %param.13) | copy-start | bytes 1179652
  53.0 9.0 %collective-permute-start.5 = (f32[2,2,160,128]{3,2,1,0:T(8,128)S(1)}, f32[2,2,160,128]{3,2,1,0:T(8,128)S(1)}, u32[]{:S(2)}, u32[]{:S(2)}) collective-permute-start(f32[2,2,160,128]{3,2,1,0:T(8,128)S(1)} %slice.137), channel_id=1, source_target_pairs={{0,1},{1,2},{2,3},{4,5},{5,6},{6,7},{8,9},{9,10},{10,11},{12,13},{... | collective-permute-start | bytes 983048 | tf_op jit(solution)/shard_map/ppermute | solution.py:12
  63.4 9.4 %collective-permute-start.6 = (f32[4,1,160,128]{3,2,1,0:T(8,128)S(1)}, f32[4,1,160,128]{3,2,1,0:T(8,128)S(1)}, u32[]{:S(2)}, u32[]{:S(2)}) collective-permute-start(f32[4,1,160,128]{3,2,1,0:T(8,128)S(1)} %slice.138), channel_id=1, source_target_pairs={{0,4},{4,8},{8,12},{12,16},{16,20},{20,24},{24,28},{1,5},{5,9},{9,... | collective-permute-start | bytes 983048 | tf_op jit(solution)/shard_map/ppermute | solution.py:12
  73.7 0.7 copy-start.11
  76.5 18.3 %copy-start.12 = (f32[256]{0:T(256)S(1)}, f32[256]{0:T(256)}, u32[]{:S(2)}) copy-start(f32[256]{0:T(256)} %param.15) | copy-start | bytes 3076
  76.7 18.2 %copy-start.6 = (f32[256,256]{1,0:T(8,128)S(1)}, f32[256,256]{1,0:T(8,128)}, u32[]{:S(2)}) copy-start(f32[256,256]{1,0:T(8,128)} %param.18) | copy-start | bytes 786436
  76.8 18.6 %copy-start.7 = (f32[256,256]{1,0:T(8,128)S(1)}, f32[256,256]{1,0:T(8,128)}, u32[]{:S(2)}) copy-start(f32[256,256]{1,0:T(8,128)} %param.17) | copy-start | bytes 786436
  94.7 1.2 %copy-start.8 = (f32[256,256]{1,0:T(8,128)S(1)}, f32[256,256]{1,0:T(8,128)}, u32[]{:S(2)}) copy-start(f32[256,256]{1,0:T(8,128)} %param.16) | copy-start | bytes 786436
  95.9 1.8 %collective-permute-start.7 = (f32[320,256]{1,0:T(8,128)S(1)}, f32[320,256]{1,0:T(8,128)S(1)}, u32[]{:S(2)}, u32[]{:S(2)}) collective-permute-start(f32[320,256]{1,0:T(8,128)S(1)} %fusion.58), channel_id=1, source_target_pairs={{0,4},{4,0},{8,12},{12,8},{16,20},{20,16},{24,28},{28,24},{1,5},{5... | collective-permute-start | bytes 983048 | tf_op jit(solution)/shard_map/ppermute | solution.py:33
  96.4 3.3 %collective-permute-start.8 = (f32[320,256]{1,0:T(8,128)S(1)}, f32[320,256]{1,0:T(8,128)S(1)}, u32[]{:S(2)}, u32[]{:S(2)}) collective-permute-start(f32[320,256]{1,0:T(8,128)S(1)} %fusion.59), channel_id=1, source_target_pairs={{0,4},{4,0},{8,12},{12,8},{16,20},{20,16},{24,28},{28,24},{1,5},{5... | collective-permute-start | bytes 983048 | tf_op jit(solution)/shard_map/ppermute | solution.py:33
  98.5 2.2 %copy-start.9 = (f32[256,256]{1,0:T(8,128)S(1)}, f32[256,256]{1,0:T(8,128)}, u32[]{:S(2)}) copy-start(f32[256,256]{1,0:T(8,128)} %param.19) | copy-start | bytes 786436
where the time goes:
time: 102 us
  starting transfers between devices  29.3 us (29%)
  matrix products  22.6 us (22%)
  waiting for transfers between devices  17.8 us (17%)
  blocking collectives  17.8 us (17%)
  local copies, waits for them, and re-layouts  8.5 us (8%)
  other arithmetic  5.25 us (5%)
    all_to_all x1, blocking collectives, local(): lax.all_to_all(pieces, 'tile', split_axis=0, concat_axis=0, tiled=True)  17.8 us
    ppermute x3, starting transfers between devices, passed_along(): return lax.ppermute(shard, axis, pairs)  16.3 us
    conv_general_dilated x2, matrix products, conv_rows(): lax.conv_general_dilated(inputs, kernel, (1, 1), ((0, 0), (1, 1)), dimens...  10.6 us
    ppermute x2, starting transfers between devices, extended(): lax.ppermute(tail, axis, [(i, (i + 1) % count) for i in range(ends)])  9.63 us
    ppermute x2, waiting for transfers between devices, extended(): lax.ppermute(head, axis, [((i + 1) % count, i) for i in range(ends)])  9.07 us
    ppermute x3, waiting for transfers between devices, passed_along(): return lax.ppermute(shard, axis, pairs)  8.69 us
    unnamed x30, local copies, waits for them, and re-layouts  4.61 us
    ppermute x2, starting transfers between devices, extended(): lax.ppermute(head, axis, [((i + 1) % count, i) for i in range(ends)])  2.76 us
  transfers between devices with their start and end apart: 9, of which 5 were waited for; matrix products, arithmetic and copies ran while one was open for 4% of the time, Pallas kernels for 0%

commit v1 on v0

--- a/solution.py
+++ b/solution.py
@@ -1,9 +1,32 @@
+import functools
 import jax
 import jax.numpy as jnp
 from jax import lax
 from jax.sharding import PartitionSpec as P
 
 highest = lax.Precision.HIGHEST
+
+
+def seats_all_hold(local_array, comm_axis):
+    e_next = lax.axis_size(comm_axis)
+    carry_in, low = (e_next, lax.axis_index(comm_axis))
+    e_now = local_array.shape[0] // carry_in
+    y2 = jnp.roll(local_array, -low * e_now, axis=0)
+    met_up = lax.slice_in_dim(y2, 0, e_now, axis=0)
+    tray = [met_up]
+    for tick in [*range(1, carry_in)]:
+        frame_out = lax.slice_in_dim(y2, tick * e_now, (tick + 1) * e_now, axis=0)
+        tray.append(
+            lax.ppermute(
+                frame_out,
+                axis_name=comm_axis,
+                perm=[(dd, (dd + tick) % carry_in) for dd in range(carry_in)],
+            )
+        )
+    return jnp.roll(jnp.concatenate(tray[::-1], axis=0), (low + 1) * tray[0].shape[0], axis=0)
+
+
+draw_task = functools.partial(seats_all_hold, comm_axis="tile")
 
 
 def passed_along(shard, axis, by):
@@ -107,9 +130,7 @@
     outer = lowered.shape[-1]
     group = tiles // frames_dev
     pieces = lowered.reshape(frames_dev * group, -1, outer)
-    mine = lax.all_to_all(pieces, "tile", split_axis=0, concat_axis=0, tiled=True).reshape(
-        -1, outer
-    )
+    mine = draw_task(pieces).reshape(-1, outer)
     normed = norm(mine, attn_gain)
     query = jnp.dot(normed, w_query, precision=highest) * float(outer) ** (-0.5)
     count = mine.shape[0]

time: 102 us -> 103 us (level)
  blocking collectives: 17.8 us -> 0 us
  starting transfers between devices: 29.3 us -> 42.8 us
  waiting for transfers between devices: 17.8 us -> 22 us
    all_to_all x1 -> x0, blocking collectives: 17.8 us -> none  [local(): lax.all_to_all(pieces, 'tile', split_axis=0, concat_axis=0, tiled=True)]
    ppermute x0 -> x7, starting transfers between devices: none -> 13.5 us  [seats_all_hold(): lax.ppermute(frame_out, axis_name=comm_axis, perm=[(dd, (dd + tick) % car...]
    ppermute x0 -> x7, waiting for transfers between devices: none -> 4.26 us  [seats_all_hold(): lax.ppermute(frame_out, axis_name=comm_axis, perm=[(dd, (dd + tick) % car...]
    unnamed x30 -> x35, local copies, waits for them, and re-layouts: 4.61 us -> 4.63 us
  transfers between devices with their start and end apart: 9 -> 16, of which waited for: 5 -> 8; matrix products, arithmetic and copies ran while one was open for 4% -> 5% of each run, Pallas kernels for 0% -> 0%
where the time goes in v1:
time: 103 us; the launch traced here: 102 us
  starting transfers between devices  42.8 us (42%)
  matrix products  22.6 us (22%)
  waiting for transfers between devices  22 us (21%)
  local copies, waits for them, and re-layouts  8.56 us (8%)
  other arithmetic  5.35 us (5%)
    ppermute x3, starting transfers between devices, passed_along(): return lax.ppermute(shard, axis, pairs)  16.3 us
    ppermute x7, starting transfers between devices, seats_all_hold(): lax.ppermute(frame_out, axis_name=comm_axis, perm=[(dd, (dd + tick) % car...  13.5 us
    conv_general_dilated x2, matrix products, conv_rows(): lax.conv_general_dilated(inputs, kernel, (1, 1), ((0, 0), (1, 1)), dimens...  10.6 us
    ppermute x2, starting transfers between devices, extended(): lax.ppermute(tail, axis, [(i, (i + 1) % count) for i in range(ends)])  9.62 us
    ppermute x2, waiting for transfers between devices, extended(): lax.ppermute(head, axis, [((i + 1) % count, i) for i in range(ends)])  9.08 us
    ppermute x3, waiting for transfers between devices, passed_along(): return lax.ppermute(shard, axis, pairs)  8.67 us
    unnamed x35, local copies, waits for them, and re-layouts  4.63 us
    ppermute x7, waiting for transfers between devices, seats_all_hold(): lax.ppermute(frame_out, axis_name=comm_axis, perm=[(dd, (dd + tick) % car...  4.26 us
  transfers between devices with their start and end apart: 16, of which 8 were waited for; matrix products, arithmetic and copies ran while one was open for 5% of the time, Pallas kernels for 0%

profile of v1, /device:TPU:0, one launch (start us, length us, event | category | flops | bytes accessed | tf_op | source)
XLA Modules:
  0.0 102.1 jit_solution(9832999053506938471)
XLA Ops:
  0.0 0.8 slice_bitcast_fusion.2
  0.8 1.4 %multiply_reduce_fusion.3 = f32[4,2,160]{2,1,0:T(2,128)S(1)} fusion(f32[4,2,160,128]{3,2,1,0:T(8,128)} %param.12), kind=kLoop, calls=%fused_computation.53 | loop fusion | flops 326400 | bytes 660480 | tf_op jit(solution)/shard_map/reduce_sum | solution.py:60
  2.3 1.3 %divide_multiply_fusion.3 = f32[4,2,160,128]{3,2,1,0:T(8,128)S(1)} fusion(f32[4,2,160,128]{3,2,1,0:T(8,128)} %param.12, f32[128]{0:T(128)S(1)} %get-tuple-element.24, f32[4,2,160]{2,1,0:T(2,128)S(1)} %add_rsqrt_fusion.3), kind=kLoop, calls=%fused_computation.52 | loop fusion | flops 983040 | bytes 1316352 | tf_op jit(solution)/shard_map/jit(silu)/mul | solution.py:64
  3.7 2.4 %collective-permute-start = (f32[4,1,160,128]{3,2,1,0:T(8,128)S(1)}, f32[4,1,160,128]{3,2,1,0:T(8,128)S(1)}, u32[]{:S(2)}, u32[]{:S(2)}) collective-permute-start(f32[4,1,160,128]{3,2,1,0:T(8,128)S(1)} %get-tuple-element.12), channel_id=1, source_target_pairs={{0,4},{4,8},{8,12},{12,16},{16,20},{20,24},{24,28},{1,5},{5,9},{9,... | collective-permute-start | bytes 983048 | tf_op jit(solution)/shard_map/ppermute | solution.py:46
  6.1 1.3 %collective-permute-start.1 = (f32[4,1,160,128]{3,2,1,0:T(8,128)S(1)}, f32[4,1,160,128]{3,2,1,0:T(8,128)S(1)}, u32[]{:S(2)}, u32[]{:S(2)}) collective-permute-start(f32[4,1,160,128]{3,2,1,0:T(8,128)S(1)} %get-tuple-element.13), channel_id=1, source_target_pairs={{4,0},{8,4},{12,8},{16,12},{20,16},{24,20},{28,24},{5,1},{9,5},{13... | collective-permute-start | bytes 983048 | tf_op jit(solution)/shard_map/ppermute | solution.py:48
  7.4 4.3 %collective-permute-done.1 = f32[4,1,160,128]{3,2,1,0:T(8,128)S(1)} collective-permute-done((f32[4,1,160,128]{3,2,1,0:T(8,128)S(1)}, f32[4,1,160,128]{3,2,1,0:T(8,128)S(1)}, u32[]{:S(2)}, u32[]{:S(2)}) %collective-permute-start.1) | collective-permute-done | bytes 327712 | tf_op jit(solution)/shard_map/ppermute | solution.py:48
  11.8 0.8 copy.52
  13.3 0.9 copy-done.2
  14.2 5.3 %multiply_reduce_fusion.1 = (f32[2,32,21]{1,2,0:T(8,128)S(1)}, f32[2,32,21,128]{3,1,2,0:T(8,128)S(1)}) fusion(f32[2,3,3,128,128]{4,3,2,1,0:T(8,128)S(1)} %copy-done.2, f32[4,4,8,23,128]{4,1,3,2,0:T(4,128)S(1)} %select_maximum_fusion.1, pred[32,21]{0,1:T(8,128)(4,1)S(1)} %copy-done.9), kind=kOutput, calls=%fused_computation.37 | convolution fusion | flops 2378685184 | bytes 2793728 | tf_op jit(solution)/shard_map/conv_general_dilated | solution.py:68
  19.5 0.5 copy.30
  20.6 3.5 %collective-permute-start.2 = (f32[2,2,160,128]{3,2,1,0:T(8,128)S(1)}, f32[2,2,160,128]{3,2,1,0:T(8,128)S(1)}, u32[]{:S(2)}, u32[]{:S(2)}) collective-permute-start(f32[2,2,160,128]{3,2,1,0:T(8,128)S(1)} %slice.162), channel_id=1, source_target_pairs={{0,1},{1,2},{2,3},{4,5},{5,6},{6,7},{8,9},{9,10},{10,11},{12,13},{... | collective-permute-start | bytes 983048 | tf_op jit(solution)/shard_map/ppermute | solution.py:35
  24.2 0.7 fusion.42
  24.9 3.8 %collective-permute-done.2 = f32[2,2,160,128]{3,2,1,0:T(8,128)S(1)} collective-permute-done((f32[2,2,160,128]{3,2,1,0:T(8,128)S(1)}, f32[2,2,160,128]{3,2,1,0:T(8,128)S(1)}, u32[]{:S(2)}, u32[]{:S(2)}) %collective-permute-start.2) | collective-permute-done | bytes 327712 | tf_op jit(solution)/shard_map/ppermute | solution.py:35
  28.7 0.7 fusion.22
  29.4 0.9 multiply_reduce_fusion.2
  30.6 7.2 %collective-permute-start.3 = (f32[4,1,160,128]{3,2,1,0:T(8,128)S(1)}, f32[4,1,160,128]{3,2,1,0:T(8,128)S(1)}, u32[]{:S(2)}, u32[]{:S(2)}) collective-permute-start(f32[4,1,160,128]{3,2,1,0:T(8,128)S(1)} %get-tuple-element.10), channel_id=1, source_target_pairs={{0,4},{4,8},{8,12},{12,16},{16,20},{20,24},{24,28},{1,5},{5,9},{9,... | collective-permute-start | bytes 983048 | tf_op jit(solution)/shard_map/ppermute | solution.py:46
  37.8 1.5 %collective-permute-start.4 = (f32[4,1,160,128]{3,2,1,0:T(8,128)S(1)}, f32[4,1,160,128]{3,2,1,0:T(8,128)S(1)}, u32[]{:S(2)}, u32[]{:S(2)}) collective-permute-start(f32[4,1,160,128]{3,2,1,0:T(8,128)S(1)} %get-tuple-element.11), channel_id=1, source_target_pairs={{4,0},{8,4},{12,8},{16,12},{20,16},{24,20},{28,24},{5,1},{9,5},{13... | collective-permute-start | bytes 983048 | tf_op jit(solution)/shard_map/ppermute | solution.py:48
  39.3 4.8 %collective-permute-done.4 = f32[4,1,160,128]{3,2,1,0:T(8,128)S(1)} collective-permute-done((f32[4,1,160,128]{3,2,1,0:T(8,128)S(1)}, f32[4,1,160,128]{3,2,1,0:T(8,128)S(1)}, u32[]{:S(2)}, u32[]{:S(2)}) %collective-permute-start.4) | collective-permute-done | bytes 327712 | tf_op jit(solution)/shard_map/ppermute | solution.py:48
  44.2 0.8 copy.53
  45.7 0.9 copy-done.3
  46.6 5.3 %multiply_reduce_fusion = (f32[2,32,21]{1,2,0:T(8,128)S(1)}, f32[2,32,21,128]{3,1,2,0:T(8,128)S(1)}) fusion(f32[2,3,3,128,128]{4,3,2,1,0:T(8,128)S(1)} %copy-done.3, f32[4,4,8,23,128]{4,1,3,2,0:T(4,128)S(1)} %select_maximum_fusion, pred[32,21]{0,1:T(8,128)(4,1)S(1)} %copy-done.9), kind=kOutput, calls=%fused_computation.36 | convolution fusion | flops 2378685184 | bytes 2793728 | tf_op jit(solution)/shard_map/conv_general_dilated | solution.py:68
  51.9 0.5 copy.36
  53.0 4.4 %collective-permute-start.5 = (f32[2,2,160,128]{3,2,1,0:T(8,128)S(1)}, f32[2,2,160,128]{3,2,1,0:T(8,128)S(1)}, u32[]{:S(2)}, u32[]{:S(2)}) collective-permute-start(f32[2,2,160,128]{3,2,1,0:T(8,128)S(1)} %slice.169), channel_id=1, source_target_pairs={{0,1},{1,2},{2,3},{4,5},{5,6},{6,7},{8,9},{9,10},{10,11},{12,13},{... | collective-permute-start | bytes 983048 | tf_op jit(solution)/shard_map/ppermute | solution.py:35
  57.4 0.7 fusion.38
  58.1 3.9 %collective-permute-done.5 = f32[2,2,160,128]{3,2,1,0:T(8,128)S(1)} collective-permute-done((f32[2,2,160,128]{3,2,1,0:T(8,128)S(1)}, f32[2,2,160,128]{3,2,1,0:T(8,128)S(1)}, u32[]{:S(2)}, u32[]{:S(2)}) %collective-permute-start.5) | collective-permute-done | bytes 327712 | tf_op jit(solution)/shard_map/ppermute | solution.py:35
  62.0 0.7 fusion.21
  62.7 0.7 fusion.15
  63.4 8.4 %collective-permute-start.6 = (f32[4,1,160,128]{3,2,1,0:T(8,128)S(1)}, f32[4,1,160,128]{3,2,1,0:T(8,128)S(1)}, u32[]{:S(2)}, u32[]{:S(2)}) collective-permute-start(f32[4,1,160,128]{3,2,1,0:T(8,128)S(1)} %slice.170), channel_id=1, source_target_pairs={{0,4},{4,8},{8,12},{12,16},{16,20},{20,24},{24,28},{1,5},{5,9},{9,... | collective-permute-start | bytes 983048 | tf_op jit(solution)/shard_map/ppermute | solution.py:35
  71.8 1.0 collective-permute-done.6
  72.9 0.6 copy.54
  74.4 1.7 %convolution_select_fusion = f32[1,32,11,256]{3,1,2,0:T(8,128)S(1)} fusion(f32[3,3,128,256]{3,2,1,0:T(8,128)S(1)} %copy-done, f32[3,4,8,24,128]{4,1,3,2,0:T(4,128)S(1)} %select_maximum_fusion.2, pred[32,11]{0,1:T(8,128)(4,1)S(1)} %copy-done.10), kind=kOutput, calls=%fused_computation.19 | convolution fusion | flops 1245798400 | bytes 2720096 | tf_op jit(solution)/shard_map/conv_general_dilated | solution.py:122
  76.1 0.4 copy.42
  77.0 6.2 %collective-permute-start.8 = (f32[1,40,256]{2,1,0:T(8,128)S(1)}, f32[1,40,256]{2,1,0:T(8,128)S(1)}, u32[]{:S(2)}, u32[]{:S(2)}) collective-permute-start(f32[1,40,256]{2,1,0:T(8,128)S(1)} %get-tuple-element.19), channel_id=1, source_target_pairs={{0,24},{4,28},{8,0},{12,4},{16,8},{20,12},{24,16},{28,20},{1,25},{... | collective-permute-start | bytes 122888 | tf_op jit(solution)/shard_map/ppermute | solution.py:20
  83.2 3.9 %collective-permute-start.9 = (f32[1,40,256]{2,1,0:T(8,128)S(1)}, f32[1,40,256]{2,1,0:T(8,128)S(1)}, u32[]{:S(2)}, u32[]{:S(2)}) collective-permute-start(f32[1,40,256]{2,1,0:T(8,128)S(1)} %get-tuple-element.18), channel_id=1, source_target_pairs={{0,20},{4,24},{8,28},{12,0},{16,4},{20,8},{24,12},{28,16},{1,21},{... | collective-permute-start | bytes 122888 | tf_op jit(solution)/shard_map/ppermute | solution.py:20
  87.3 1.5 %collective-permute-start.11 = (f32[1,40,256]{2,1,0:T(8,128)S(1)}, f32[1,40,256]{2,1,0:T(8,128)S(1)}, u32[]{:S(2)}, u32[]{:S(2)}) collective-permute-start(f32[1,40,256]{2,1,0:T(8,128)S(1)} %get-tuple-element.16), channel_id=1, source_target_pairs={{0,12},{4,16},{8,20},{12,24},{16,28},{20,0},{24,4},{28,8},{1,13},{... | collective-permute-start | bytes 122888 | tf_op jit(solution)/shard_map/ppermute | solution.py:20
  88.8 1.6 %collective-permute-start.12 = (f32[1,40,256]{2,1,0:T(8,128)S(1)}, f32[1,40,256]{2,1,0:T(8,128)S(1)}, u32[]{:S(2)}, u32[]{:S(2)}) collective-permute-start(f32[1,40,256]{2,1,0:T(8,128)S(1)} %get-tuple-element.15), channel_id=1, source_target_pairs={{0,8},{4,12},{8,16},{12,20},{16,24},{20,28},{24,0},{28,4},{1,9},{5... | collective-permute-start | bytes 122888 | tf_op jit(solution)/shard_map/ppermute | solution.py:20
  90.5 1.0 %collective-permute-done.10 = f32[1,40,256]{2,1,0:T(8,128)S(1)} collective-permute-done((f32[1,40,256]{2,1,0:T(8,128)S(1)}, f32[1,40,256]{2,1,0:T(8,128)S(1)}, u32[]{:S(2)}, u32[]{:S(2)}) %collective-permute-start.10) | collective-permute-done | bytes 40992 | tf_op jit(solution)/shard_map/ppermute | solution.py:20
  91.5 2.2 %collective-permute-done.12 = f32[1,40,256]{2,1,0:T(8,128)S(1)} collective-permute-done((f32[1,40,256]{2,1,0:T(8,128)S(1)}, f32[1,40,256]{2,1,0:T(8,128)S(1)}, u32[]{:S(2)}, u32[]{:S(2)}) %collective-permute-start.12) | collective-permute-done | bytes 40992 | tf_op jit(solution)/shard_map/ppermute | solution.py:20
  93.7 1.1 %collective-permute-done.13 = f32[1,40,256]{2,1,0:T(8,128)S(1)} collective-permute-done((f32[1,40,256]{2,1,0:T(8,128)S(1)}, f32[1,40,256]{2,1,0:T(8,128)S(1)}, u32[]{:S(2)}, u32[]{:S(2)}) %collective-permute-start.13) | collective-permute-done | bytes 40992 | tf_op jit(solution)/shard_map/ppermute | solution.py:20
  95.2 0.4 fusion.62
  95.7 0.4 convolution_multiply_fusion
  96.1 0.4 fusion.63
  96.6 0.6 collective-permute-start.15
  97.1 0.7 fusion.60
  97.8 0.7 fusion.61
  98.7 1.1 %fusion.17 = f32[320,256]{1,0:T(8,128)S(1)} fusion(f32[320,256]{1,0:T(8,128)S(1)} %fusion.63, f32[320,320]{0,1:T(8,128)S(1)} %get-tuple-element.33, f32[320]{0:T(512)S(1)} %get-tuple-element.32, f32[320]{0:T(512)S(1)} %get-tuple-element.7, f32[320]{0:T(512)S(1)} %get-tuple-element.21), kind=kOutput, calls=%fused_computation.25 | convolution fusion | flops 314839040 | bytes 1068800 | tf_op jit(solution)/shard_map/dot_general | solution.py:97
  99.8 1.1 %fusion.18 = f32[320,256]{1,0:T(8,128)S(1)} fusion(f32[320,256]{1,0:T(8,128)S(1)} %fusion.17, f32[320,256]{1,0:T(8,128)S(1)} %collective-permute-done.15, f32[320,320]{0,1:T(8,128)S(1)} %get-tuple-element.35, f32[320]{0:T(512)S(1)} %max.13, f32[320]{0:T(512)S(1)} %get-tuple-element.6), kind=kOutput, calls=%fused_computation.26 | convolution fusion | flops 314839040 | bytes 1395200 | tf_op jit(solution)/shard_map/dot_general | solution.py:97
  100.9 1.2 %fusion.16 = f32[1,320,256]{2,1,0:T(8,128)} fusion(f32[320,256]{1,0:T(8,128)S(1)} %bitcast.141, f32[320,256]{1,0:T(8,128)S(1)} %fusion.18, f32[256,256]{1,0:T(8,128)S(1)} %copy-done.8), kind=kOutput, calls=%fused_computation.21 | convolution fusion | flops 251740160 | bytes 1245184 | tf_op jit(solution)/shard_map/dot_general | solution.py:153
  (91 shorter events, 5.1 us)
Async XLA Ops:
  0.0 74.0 %copy-start = (f32[3,3,128,256]{3,2,1,0:T(8,128)S(1)}, f32[3,3,128,256]{3,2,1,0:T(8,128)}, u32[]{:S(2)}) copy-start(f32[3,3,128,256]{3,2,1,0:T(8,128)} %param.16) | copy-start | bytes 3538948
  3.7 3.7 %collective-permute-start = (f32[4,1,160,128]{3,2,1,0:T(8,128)S(1)}, f32[4,1,160,128]{3,2,1,0:T(8,128)S(1)}, u32[]{:S(2)}, u32[]{:S(2)}) collective-permute-start(f32[4,1,160,128]{3,2,1,0:T(8,128)S(1)} %get-tuple-element.12), channel_id=1, source_target_pairs={{0,4},{4,8},{8,12},{12,16},{16,20},{20,24},{24,28},{1,5},{5,9},{9,... | collective-permute-start | bytes 983048 | tf_op jit(solution)/shard_map/ppermute | solution.py:46
  6.1 5.6 %collective-permute-start.1 = (f32[4,1,160,128]{3,2,1,0:T(8,128)S(1)}, f32[4,1,160,128]{3,2,1,0:T(8,128)S(1)}, u32[]{:S(2)}, u32[]{:S(2)}) collective-permute-start(f32[4,1,160,128]{3,2,1,0:T(8,128)S(1)} %get-tuple-element.13), channel_id=1, source_target_pairs={{4,0},{8,4},{12,8},{16,12},{20,16},{24,20},{28,24},{5,1},{9,5},{13... | collective-permute-start | bytes 983048 | tf_op jit(solution)/shard_map/ppermute | solution.py:48
  12.9 1.3 %copy-start.2 = (f32[2,3,3,128,128]{4,3,2,1,0:T(8,128)S(1)}, f32[2,3,3,128,128]{4,3,2,1,0:T(8,128)}, u32[]{:S(2)}) copy-start(f32[2,3,3,128,128]{4,3,2,1,0:T(8,128)} %param.14) | copy-start | bytes 3538948
  12.9 1.3 %copy-start.9 = (pred[32,21]{0,1:T(8,128)(4,1)S(1)}, pred[32,21]{0,1:T(8,128)(4,1)}, u32[]{:S(2)}) copy-start(pred[32,21]{0,1:T(8,128)(4,1)} %constant.71) | copy-start | bytes 2020
  20.1 4.1 %copy-start.4 = (f32[2,3,128,128]{3,2,1,0:T(8,128)S(1)}, f32[2,3,128,128]{3,2,1,0:T(8,128)}, u32[]{:S(2)}) copy-start(f32[2,3,128,128]{3,2,1,0:T(8,128)} %param.15) | copy-start | bytes 1179652
  20.6 8.1 %collective-permute-start.2 = (f32[2,2,160,128]{3,2,1,0:T(8,128)S(1)}, f32[2,2,160,128]{3,2,1,0:T(8,128)S(1)}, u32[]{:S(2)}, u32[]{:S(2)}) collective-permute-start(f32[2,2,160,128]{3,2,1,0:T(8,128)S(1)} %slice.162), channel_id=1, source_target_pairs={{0,1},{1,2},{2,3},{4,5},{5,6},{6,7},{8,9},{9,10},{10,11},{12,13},{... | collective-permute-start | bytes 983048 | tf_op jit(solution)/shard_map/ppermute | solution.py:35
  24.8 4.6 %copy-start.1 = (f32[4,2,160,128]{3,2,1,0:T(8,128)S(1)}, f32[4,2,160,128]{3,2,1,0:T(8,128)}, u32[]{:S(2)}) copy-start(f32[4,2,160,128]{3,2,1,0:T(8,128)} %param.12) | copy-start | bytes 1966084
  30.6 8.7 %collective-permute-start.3 = (f32[4,1,160,128]{3,2,1,0:T(8,128)S(1)}, f32[4,1,160,128]{3,2,1,0:T(8,128)S(1)}, u32[]{:S(2)}, u32[]{:S(2)}) collective-permute-start(f32[4,1,160,128]{3,2,1,0:T(8,128)S(1)} %get-tuple-element.10), channel_id=1, source_target_pairs={{0,4},{4,8},{8,12},{12,16},{16,20},{20,24},{24,28},{1,5},{5,9},{9,... | collective-permute-start | bytes 983048 | tf_op jit(solution)/shard_map/ppermute | solution.py:46
  37.8 6.3 %collective-permute-start.4 = (f32[4,1,160,128]{3,2,1,0:T(8,128)S(1)}, f32[4,1,160,128]{3,2,1,0:T(8,128)S(1)}, u32[]{:S(2)}, u32[]{:S(2)}) collective-permute-start(f32[4,1,160,128]{3,2,1,0:T(8,128)S(1)} %get-tuple-element.11), channel_id=1, source_target_pairs={{4,0},{8,4},{12,8},{16,12},{20,16},{24,20},{28,24},{5,1},{9,5},{13... | collective-permute-start | bytes 983048 | tf_op jit(solution)/shard_map/ppermute | solution.py:48
  45.3 1.3 %copy-start.3 = (f32[2,3,3,128,128]{4,3,2,1,0:T(8,128)S(1)}, f32[2,3,3,128,128]{4,3,2,1,0:T(8,128)}, u32[]{:S(2)}) copy-start(f32[2,3,3,128,128]{4,3,2,1,0:T(8,128)} %param.14) | copy-start | bytes 3538948
  53.0 9.0 %collective-permute-start.5 = (f32[2,2,160,128]{3,2,1,0:T(8,128)S(1)}, f32[2,2,160,128]{3,2,1,0:T(8,128)S(1)}, u32[]{:S(2)}, u32[]{:S(2)}) collective-permute-start(f32[2,2,160,128]{3,2,1,0:T(8,128)S(1)} %slice.169), channel_id=1, source_target_pairs={{0,1},{1,2},{2,3},{4,5},{5,6},{6,7},{8,9},{9,10},{10,11},{12,13},{... | collective-permute-start | bytes 983048 | tf_op jit(solution)/shard_map/ppermute | solution.py:35
  63.4 9.4 %collective-permute-start.6 = (f32[4,1,160,128]{3,2,1,0:T(8,128)S(1)}, f32[4,1,160,128]{3,2,1,0:T(8,128)S(1)}, u32[]{:S(2)}, u32[]{:S(2)}) collective-permute-start(f32[4,1,160,128]{3,2,1,0:T(8,128)S(1)} %slice.170), channel_id=1, source_target_pairs={{0,4},{4,8},{8,12},{12,16},{16,20},{20,24},{24,28},{1,5},{5,9},{9,... | collective-permute-start | bytes 983048 | tf_op jit(solution)/shard_map/ppermute | solution.py:35
  73.7 0.7 copy-start.10
  76.8 18.3 %copy-start.11 = (f32[256]{0:T(256)S(1)}, f32[256]{0:T(256)}, u32[]{:S(2)}) copy-start(f32[256]{0:T(256)} %param.17) | copy-start | bytes 3076
  76.8 18.3 %copy-start.5 = (f32[256,256]{1,0:T(8,128)S(1)}, f32[256,256]{1,0:T(8,128)}, u32[]{:S(2)}) copy-start(f32[256,256]{1,0:T(8,128)} %param.19) | copy-start | bytes 786436
  76.9 11.9 %collective-permute-start.7 = (f32[1,40,256]{2,1,0:T(8,128)S(1)}, f32[1,40,256]{2,1,0:T(8,128)S(1)}, u32[]{:S(2)}, u32[]{:S(2)}) collective-permute-start(f32[1,40,256]{2,1,0:T(8,128)S(1)} %get-tuple-element.20), channel_id=1, source_target_pairs={{0,28},{4,0},{8,4},{12,8},{16,12},{20,16},{24,20},{28,24},{1,29},{... | collective-permute-start | bytes 122888 | tf_op jit(solution)/shard_map/ppermute | solution.py:20
  77.0 13.5 %collective-permute-start.8 = (f32[1,40,256]{2,1,0:T(8,128)S(1)}, f32[1,40,256]{2,1,0:T(8,128)S(1)}, u32[]{:S(2)}, u32[]{:S(2)}) collective-permute-start(f32[1,40,256]{2,1,0:T(8,128)S(1)} %get-tuple-element.19), channel_id=1, source_target_pairs={{0,24},{4,28},{8,0},{12,4},{16,8},{20,12},{24,16},{28,20},{1,25},{... | collective-permute-start | bytes 122888 | tf_op jit(solution)/shard_map/ppermute | solution.py:20
  83.2 7.3 %collective-permute-start.9 = (f32[1,40,256]{2,1,0:T(8,128)S(1)}, f32[1,40,256]{2,1,0:T(8,128)S(1)}, u32[]{:S(2)}, u32[]{:S(2)}) collective-permute-start(f32[1,40,256]{2,1,0:T(8,128)S(1)} %get-tuple-element.18), channel_id=1, source_target_pairs={{0,20},{4,24},{8,28},{12,0},{16,4},{20,8},{24,12},{28,16},{1,21},{... | collective-permute-start | bytes 122888 | tf_op jit(solution)/shard_map/ppermute | solution.py:20
  87.1 4.4 %collective-permute-start.10 = (f32[1,40,256]{2,1,0:T(8,128)S(1)}, f32[1,40,256]{2,1,0:T(8,128)S(1)}, u32[]{:S(2)}, u32[]{:S(2)}) collective-permute-start(f32[1,40,256]{2,1,0:T(8,128)S(1)} %get-tuple-element.17), channel_id=1, source_target_pairs={{0,16},{4,20},{8,24},{12,28},{16,0},{20,4},{24,8},{28,12},{1,17},{... | collective-permute-start | bytes 122888 | tf_op jit(solution)/shard_map/ppermute | solution.py:20
  87.3 4.2 %collective-permute-start.11 = (f32[1,40,256]{2,1,0:T(8,128)S(1)}, f32[1,40,256]{2,1,0:T(8,128)S(1)}, u32[]{:S(2)}, u32[]{:S(2)}) collective-permute-start(f32[1,40,256]{2,1,0:T(8,128)S(1)} %get-tuple-element.16), channel_id=1, source_target_pairs={{0,12},{4,16},{8,20},{12,24},{16,28},{20,0},{24,4},{28,8},{1,13},{... | collective-permute-start | bytes 122888 | tf_op jit(solution)/shard_map/ppermute | solution.py:20
  88.8 4.9 %collective-permute-start.12 = (f32[1,40,256]{2,1,0:T(8,128)S(1)}, f32[1,40,256]{2,1,0:T(8,128)S(1)}, u32[]{:S(2)}, u32[]{:S(2)}) collective-permute-start(f32[1,40,256]{2,1,0:T(8,128)S(1)} %get-tuple-element.15), channel_id=1, source_target_pairs={{0,8},{4,12},{8,16},{12,20},{16,24},{20,28},{24,0},{28,4},{1,9},{5... | collective-permute-start | bytes 122888 | tf_op jit(solution)/shard_map/ppermute | solution.py:20
  90.4 4.3 %collective-permute-start.13 = (f32[1,40,256]{2,1,0:T(8,128)S(1)}, f32[1,40,256]{2,1,0:T(8,128)S(1)}, u32[]{:S(2)}, u32[]{:S(2)}) collective-permute-start(f32[1,40,256]{2,1,0:T(8,128)S(1)} %get-tuple-element.14), channel_id=1, source_target_pairs={{0,4},{4,8},{8,12},{12,16},{16,20},{20,24},{24,28},{28,0},{1,5},{5... | collective-permute-start | bytes 122888 | tf_op jit(solution)/shard_map/ppermute | solution.py:20
  91.5 4.2 %copy-start.6 = (f32[256,256]{1,0:T(8,128)S(1)}, f32[256,256]{1,0:T(8,128)}, u32[]{:S(2)}) copy-start(f32[256,256]{1,0:T(8,128)} %param.18) | copy-start | bytes 786436
  94.9 1.2 %copy-start.7 = (f32[256,256]{1,0:T(8,128)S(1)}, f32[256,256]{1,0:T(8,128)}, u32[]{:S(2)}) copy-start(f32[256,256]{1,0:T(8,128)} %param.20) | copy-start | bytes 786436
  95.6 2.2 %collective-permute-start.14 = (f32[320,256]{1,0:T(8,128)S(1)}, f32[320,256]{1,0:T(8,128)S(1)}, u32[]{:S(2)}, u32[]{:S(2)}) collective-permute-start(f32[320,256]{1,0:T(8,128)S(1)} %fusion.62), channel_id=1, source_target_pairs={{0,4},{4,0},{8,12},{12,8},{16,20},{20,16},{24,28},{28,24},{1,5},{5... | collective-permute-start | bytes 983048 | tf_op jit(solution)/shard_map/ppermute | solution.py:56
  96.6 3.3 %collective-permute-start.15 = (f32[320,256]{1,0:T(8,128)S(1)}, f32[320,256]{1,0:T(8,128)S(1)}, u32[]{:S(2)}, u32[]{:S(2)}) collective-permute-start(f32[320,256]{1,0:T(8,128)S(1)} %fusion.63), channel_id=1, source_target_pairs={{0,4},{4,0},{8,12},{12,8},{16,20},{20,16},{24,28},{28,24},{1,5},{5... | collective-permute-start | bytes 983048 | tf_op jit(solution)/shard_map/ppermute | solution.py:56
  98.7 2.2 %copy-start.8 = (f32[256,256]{1,0:T(8,128)S(1)}, f32[256,256]{1,0:T(8,128)}, u32[]{:S(2)}) copy-start(f32[256,256]{1,0:T(8,128)} %param.21) | copy-start | bytes 786436
